TPU v7x, 32 devices: a whole 2x2x4 slice. The times are simulated.
32 devices in a mesh: seq: 8 (over z, x), head: 4 (over y, core).
Axes of the slice: x: 2, y: 2, z: 4, core: 2. Of those that a mesh axis runs over, the one named last changes fastest.
Arguments:
- queries: bfloat16 [1024, 4096], P(('seq', 'head')), may hold values from -0.5 to 0.5
- keys: bfloat16 [1024, 4096], P(('seq', 'head')), may hold values from -0.5 to 0.5
- values: bfloat16 [1024, 4096], P(('seq', 'head')), may hold values from -6 to 6
- grad_out: bfloat16 [1024, 4096], P(('seq', 'head')), may hold values from -6 to 6
- gates: float32 [1024, 32], P('seq', 'head'), may hold values from -1.5 to 0, as said below
Outputs:
- grad_queries: bfloat16 [1024, 4096], P('seq', 'head')
- grad_keys: bfloat16 [1024, 4096], P('seq', 'head')
- grad_values: bfloat16 [1024, 4096], P('seq', 'head')
Inputs may be any that keep to these rules, and one draw needn't show every extreme that they name: gates are negative.
All inputs are finite; a program needn't handle non-finite values.
Results may differ from a plain program's by a relative error of at most 0.0058.
Values may be sent and summed in bfloat16 or wider, within the bound.
A program may use at most 128 MiB of HBM per device.

v0:
```python
import jax
import jax.numpy as jnp
from jax import lax
from jax.sharding import PartitionSpec as P

HEAD_COUNT = 32
DH = 128


HIGHEST_PRECISION = lax.Precision.HIGHEST


def entering(part, axis, combine, identity, reverse):
    count = lax.axis_size(axis)
    place = lax.axis_index(axis)
    ahead = count - 1 - place if reverse else place
    gathered = jax.tree.map(lambda a: lax.all_gather(a, axis), part)
    state = jax.tree.map(lambda a, e: jnp.zeros_like(a) + jnp.asarray(e, a.dtype), part, identity)

    def one(hop, state):
        source = count - 1 - hop if reverse else hop
        return combine(
            state, jax.tree.map(lambda a: lax.dynamic_index_in_dim(a, source, 0, False), gathered)
        )

    return lax.fori_loop(0, ahead, one, state)


def decay_parts(gate_rows):
    cumulated = jnp.cumsum(gate_rows, axis=0)
    block_end = cumulated[-1]
    by_head = cumulated.T
    position_indices = jnp.arange(cumulated.shape[0])
    causal = position_indices[:, None] >= position_indices[None, :]
    log_gaps = jnp.where(causal[None], by_head[:, :, None] - by_head[:, None, :], 0.0)
    decay_table = jnp.where(causal[None], jnp.exp(log_gaps), 0.0)
    return (cumulated, block_end, decay_table)


def chain_step(earlier, following):
    return (earlier[0] * following[0], following[0][:, None, None] * earlier[1] + following[1])


def joined_step(earlier, following):
    return (
        earlier[0] * following[0],
        following[0][:, None, None] * earlier[1] + following[1],
        following[0] * earlier[2] + following[2],
    )


def body(queries, keys, values, grad_out, gates):
    row_count = queries.shape[0]
    split_queries = queries.reshape(row_count, HEAD_COUNT, DH)
    split_keys = keys.reshape(row_count, HEAD_COUNT, DH)
    split_values = values.reshape(row_count, HEAD_COUNT, DH)
    split_grads = grad_out.reshape(row_count, HEAD_COUNT, DH)
    query_rows, key_rows, value_rows, grad_rows = (
        lax.all_to_all(split_queries, "head", split_axis=1, concat_axis=0, tiled=True),
        lax.all_to_all(split_keys, "head", split_axis=1, concat_axis=0, tiled=True),
        lax.all_to_all(split_values, "head", split_axis=1, concat_axis=0, tiled=True),
        lax.all_to_all(split_grads, "head", split_axis=1, concat_axis=0, tiled=True),
    )
    cumulated, block_end, decay_table = decay_parts(gates)
    growth = jnp.exp(cumulated)
    fade_out = jnp.exp(block_end[None, :] - cumulated)
    carry_gain = jnp.exp(block_end)
    key_fade = key_rows.astype(jnp.float32) * fade_out[:, :, None]
    local_state = jnp.einsum(
        "thd,the->hde", key_fade, value_rows.astype(jnp.float32), precision=HIGHEST_PRECISION
    )
    local_norm = jnp.sum(fade_out, axis=0)
    unit_gain = jnp.ones_like(carry_gain)
    zero_state = jnp.zeros_like(local_state)
    zero_norm = jnp.zeros_like(local_norm)
    unused_gain, prefix_state, prefix_norm = entering(
        (carry_gain, local_state, local_norm),
        "seq",
        joined_step,
        (unit_gain, zero_state, zero_norm),
        False,
    )
    norm_total = growth * prefix_norm[None, :] + jnp.sum(decay_table, axis=2).T
    inverse_root = lax.rsqrt(norm_total)
    scaled = (grad_rows.astype(jnp.float32) * inverse_root[:, :, None]).astype(jnp.bfloat16)
    query_growth = query_rows.astype(jnp.float32) * growth[:, :, None]
    reach = jnp.einsum(
        "thd,the->hde", query_growth, scaled.astype(jnp.float32), precision=HIGHEST_PRECISION
    )
    unused_back, later_state = entering(
        (carry_gain, reach), "seq", chain_step, (unit_gain, zero_state), True
    )
    mixing = jnp.einsum("the,she->hts", grad_rows, value_rows, preferred_element_type=jnp.float32)
    weighted = (mixing * decay_table * inverse_root.T[:, :, None]).astype(jnp.bfloat16)
    affinity_raw = jnp.einsum(
        "thd,shd->hts", query_rows, key_rows, preferred_element_type=jnp.float32
    )
    affinity = (affinity_raw * decay_table).astype(jnp.bfloat16)
    prefix_low = prefix_state.astype(jnp.bfloat16)
    later_low = later_state.astype(jnp.bfloat16)
    grad_q = jnp.einsum("hts,shd->thd", weighted, key_rows, preferred_element_type=jnp.float32)
    grad_q = grad_q + growth[:, :, None] * jnp.einsum(
        "the,hde->thd", scaled, prefix_low, preferred_element_type=jnp.float32
    )
    grad_k = jnp.einsum("hts,thd->shd", weighted, query_rows, preferred_element_type=jnp.float32)
    grad_k = grad_k + fade_out[:, :, None] * jnp.einsum(
        "she,hde->shd", value_rows, later_low, preferred_element_type=jnp.float32
    )
    grad_v = jnp.einsum("hts,the->she", affinity, scaled, preferred_element_type=jnp.float32)
    grad_v = grad_v + fade_out[:, :, None] * jnp.einsum(
        "shd,hde->she", key_rows, later_low, preferred_element_type=jnp.float32
    )
    position_count = grad_q.shape[0]
    return (
        grad_q.reshape(position_count, -1).astype(jnp.bfloat16),
        grad_k.reshape(position_count, -1).astype(jnp.bfloat16),
        grad_v.reshape(position_count, -1).astype(jnp.bfloat16),
    )


def solution(mesh):
    placed = (
        P(("seq", "head"), None),
        P(("seq", "head"), None),
        P(("seq", "head"), None),
        P(("seq", "head"), None),
        P("seq", "head"),
    )
    return jax.shard_map(
        body,
        mesh=mesh,
        in_specs=placed,
        out_specs=(P("seq", "head"), P("seq", "head"), P("seq", "head")),
        check_vma=False,
    )
```

profile of v0, /device:TPU:0, one launch (start us, length us, event | category | flops | bytes accessed | tf_op | source)
XLA Modules:
  0.0 205.2 jit_solution(14552548037547748749)
XLA Ops:
  7.2 0.0 copy-start
  7.2 0.0 copy-start.3
  7.2 0.0 copy-start.1
  7.2 1.0 copy-done
  8.2 0.0 copy-start.2
  8.2 0.7 copy_bitcast_fusion.1
  8.9 4.2 %all-to-all-start.2 = ((bf16[32,32,128]{2,0,1:T(8,128)(2,1)}), bf16[32,32,128]{2,0,1:T(8,128)(2,1)S(1)}, u32[]{:S(2)}, u32[]{:S(2)}) async-start(bf16[32,32,128]{2,0,1:T(8,128)(2,1)} %copy_bitcast_fusion.1), calls=%async_computation.2 | async-start | bytes 524288 | tf_op jit(solution)/shard_map/all_to_all | solution.py:60
  13.2 0.8 copy.110
  14.0 1.7 copy_bitcast_fusion.2
  15.7 0.2 reduce_window_sum.11
  15.9 3.4 %all-to-all-done.2 = bf16[32,32,128]{2,0,1:T(8,128)(2,1)S(1)} async-done(((bf16[32,32,128]{2,0,1:T(8,128)(2,1)}), bf16[32,32,128]{2,0,1:T(8,128)(2,1)S(1)}, u32[]{:S(2)}, u32[]{:S(2)}) %all-to-all-start.2) | async-done | bytes 262176 | tf_op jit(solution)/shard_map/all_to_all | solution.py:60
  19.2 3.4 %all-to-all-start.1 = ((bf16[32,32,128]{2,0,1:T(8,128)(2,1)}), bf16[32,32,128]{2,0,1:T(8,128)(2,1)S(1)}, u32[]{:S(2)}, u32[]{:S(2)}) async-start(bf16[32,32,128]{2,0,1:T(8,128)(2,1)} %copy_bitcast_fusion.2), calls=%async_computation.1 | async-start | bytes 524288 | tf_op jit(solution)/shard_map/all_to_all | solution.py:61
  22.6 0.0 all-gather.7.cloned.1.call-start
  22.8 0.1 copy.114
  22.9 0.2 copy.115
  23.1 5.5 %all-to-all-done.1 = bf16[32,32,128]{2,0,1:T(8,128)(2,1)S(1)} async-done(((bf16[32,32,128]{2,0,1:T(8,128)(2,1)}), bf16[32,32,128]{2,0,1:T(8,128)(2,1)S(1)}, u32[]{:S(2)}, u32[]{:S(2)}) %all-to-all-start.1) | async-done | bytes 262176 | tf_op jit(solution)/shard_map/all_to_all | solution.py:61
  28.7 1.2 fusion.18
  29.9 0.0 all-gather.7.cloned.1.call-update
  29.9 0.0 copy-done.1
  29.9 0.7 copy_bitcast_fusion.3
  30.6 3.4 %all-to-all-start = ((bf16[32,32,128]{2,0,1:T(8,128)(2,1)}), bf16[32,32,128]{2,0,1:T(8,128)(2,1)S(1)}, u32[]{:S(2)}, u32[]{:S(2)}) async-start(bf16[32,32,128]{2,0,1:T(8,128)(2,1)} %copy_bitcast_fusion.3), calls=%async_computation | async-start | bytes 524288 | tf_op jit(solution)/shard_map/all_to_all | solution.py:62
  34.1 0.1 copy.111
  34.1 0.0 copy-done.3
  34.1 0.6 dynamic-slice
  35.4 0.2 dynamic-update-slice
  35.6 22.7 %all-reduce = f32[64]{0:T(128)S(1)} all-reduce(f32[64]{0:T(128)S(1)} %dynamic-update-slice), channel_id=3, replica_groups=mesh['seq'=8,'head'=4] {'seq'}, use_global_device_ids=true, to_apply=%add | all-reduce | flops 64 | bytes 512
  58.3 0.1 reshape.70
  58.4 0.0 copy-done.2
  58.4 0.8 copy_bitcast_fusion
  59.2 0.0 all-to-all-done
  59.2 3.4 %all-to-all-start.3 = ((bf16[32,32,128]{2,0,1:T(8,128)(2,1)}), bf16[32,32,128]{2,0,1:T(8,128)(2,1)S(1)}, u32[]{:S(2)}, u32[]{:S(2)}) async-start(bf16[32,32,128]{2,0,1:T(8,128)(2,1)} %copy_bitcast_fusion), calls=%async_computation.3 | async-start | bytes 524288 | tf_op jit(solution)/shard_map/all_to_all | solution.py:59
  62.6 0.0 all-gather.9.cloned.1.call-start
  62.7 0.4 fusion.21
  63.1 0.1 copy.119
  63.2 16.4 %all-gather.3 = f32[8,1,8]{2,1,0:T(1,128)S(1)} all-gather(f32[1,1,8]{2,1,0:T(1,128)S(1)} %get-tuple-element.195), channel_id=1, replica_groups=mesh['seq'=8,'head'=4] {'seq'}, dimensions={0}, use_global_device_ids=true | all-gather | bytes 288 | tf_op jit(solution)/shard_map/all_gather | solution.py:17
  79.6 0.0 all-to-all-done.3
  79.6 0.1 copy.123
  79.7 0.2 copy.124
  79.9 24.7 %all-gather.7.cloned.1.call-done = f32[64,128,128]{2,1,0:T(8,128)} async-done(((f32[8,128,128]{2,1,0:T(8,128)}), f32[64,128,128]{2,1,0:T(8,128)}) %all-gather.7.cloned.1.call-update) | async-done | bytes 4194320 | tf_op jit(solution)/shard_map/all_gather | solution.py:17
  104.8 0.1 copy.118
  104.8 1.4 fusion.15
  106.2 0.0 all-gather.9.cloned.1.call-update
  106.2 0.1 add_rsqrt_fusion
  106.3 0.4 fusion.10
  106.7 0.4 fusion.4
  107.1 0.3 fusion.14
  107.4 0.9 copy.131
  108.2 0.2 convolution_bitcast_fusion
  108.5 78.3 %all-gather.9.cloned.1.call-done = f32[64,128,128]{2,1,0:T(8,128)} async-done(((f32[8,128,128]{2,1,0:T(8,128)}), f32[64,128,128]{2,1,0:T(8,128)}) %all-gather.9.cloned.1.call-update) | async-done | bytes 4194320 | tf_op jit(solution)/shard_map/all_gather | solution.py:17
  186.8 8.6 %while.29 = (s32[]{:T(128)}, f32[8,128,128]{2,1,0:T(8,128)S(1)}, s32[]{:T(128)}, f32[8,8]{1,0:T(8,128)S(1)}, f32[8,8,128,128]{3,2,1,0:T(8,128)}, /*index=5*/s32[]{:T(128)}, s32[]{:T(128)}, s32[]{:T(128)}, s32[]{:T(128)}) while((s32[]{:T(128)}, f32[8,128,128]{2,1,0:T(8,128)S(1)}, s32[]{:T(128)}, f32[8,8]{1,0:T(8,128)S(1)}, ...), condition=%wide.region_6.7_spmd, body=%wide.region_5.6_spmd.sunk | while | flops 262150 | bytes 1573107 | solution.py:26
  186.8 1.2 bitcast_add_fusion.6
  188.0 1.2 bitcast_add_fusion.6
  189.3 1.2 bitcast_add_fusion.6
  190.5 1.2 bitcast_add_fusion.6
  191.7 1.2 bitcast_add_fusion.6
  193.0 1.2 bitcast_add_fusion.6
  194.2 1.2 bitcast_add_fusion.6
  195.4 0.3 fusion.8
  195.7 0.7 fusion.13
  196.4 0.9 copy.133
  197.3 0.3 fusion.11
  197.6 0.9 copy.132
  (20 shorter events, 0.4 us)
Async XLA Ops:
  7.2 1.0 copy-start
  7.2 27.0 %copy-start.3 = (u32[32]{0:T(128)S(1)}, u32[32]{0:T(128)}, u32[]{:S(2)}) copy-start(u32[32]{0:T(128)} %constant.69) | copy-start | bytes 388
  7.2 22.7 %copy-start.1 = (bf16[32,4096]{1,0:T(8,128)(2,1)S(1)}, bf16[32,4096]{1,0:T(8,128)(2,1)}, u32[]{:S(2)}) copy-start(bf16[32,4096]{1,0:T(8,128)(2,1)} %param.12) | copy-start | bytes 786436
  8.2 50.2 %copy-start.2 = (bf16[32,4096]{1,0:T(8,128)(2,1)S(1)}, bf16[32,4096]{1,0:T(8,128)(2,1)}, u32[]{:S(2)}) copy-start(bf16[32,4096]{1,0:T(8,128)(2,1)} %param.9) | copy-start | bytes 786436
  8.9 10.3 %all-to-all-start.2 = ((bf16[32,32,128]{2,0,1:T(8,128)(2,1)}), bf16[32,32,128]{2,0,1:T(8,128)(2,1)S(1)}, u32[]{:S(2)}, u32[]{:S(2)}) async-start(bf16[32,32,128]{2,0,1:T(8,128)(2,1)} %copy_bitcast_fusion.1), calls=%async_computation.2 | async-start | bytes 524288 | tf_op jit(solution)/shard_map/all_to_all | solution.py:60
  19.2 9.4 %all-to-all-start.1 = ((bf16[32,32,128]{2,0,1:T(8,128)(2,1)}), bf16[32,32,128]{2,0,1:T(8,128)(2,1)S(1)}, u32[]{:S(2)}, u32[]{:S(2)}) async-start(bf16[32,32,128]{2,0,1:T(8,128)(2,1)} %copy_bitcast_fusion.2), calls=%async_computation.1 | async-start | bytes 524288 | tf_op jit(solution)/shard_map/all_to_all | solution.py:61
  22.6 82.0 %all-gather.7.cloned.1.call-start = ((), (), s32[]{:S(2)}) async-start(), calls=%async_computation.4 | async-start | bytes 4718592 | tf_op jit(solution)/shard_map/all_gather | solution.py:17
  30.6 28.5 %all-to-all-start = ((bf16[32,32,128]{2,0,1:T(8,128)(2,1)}), bf16[32,32,128]{2,0,1:T(8,128)(2,1)S(1)}, u32[]{:S(2)}, u32[]{:S(2)}) async-start(bf16[32,32,128]{2,0,1:T(8,128)(2,1)} %copy_bitcast_fusion.3), calls=%async_computation | async-start | bytes 524288 | tf_op jit(solution)/shard_map/all_to_all | solution.py:62
  59.2 20.4 %all-to-all-start.3 = ((bf16[32,32,128]{2,0,1:T(8,128)(2,1)}), bf16[32,32,128]{2,0,1:T(8,128)(2,1)S(1)}, u32[]{:S(2)}, u32[]{:S(2)}) async-start(bf16[32,32,128]{2,0,1:T(8,128)(2,1)} %copy_bitcast_fusion), calls=%async_computation.3 | async-start | bytes 524288 | tf_op jit(solution)/shard_map/all_to_all | solution.py:59
  62.6 124.1 %all-gather.9.cloned.1.call-start = ((), (), s32[]{:S(2)}) async-start(), calls=%async_computation.5 | async-start | bytes 4718592 | tf_op jit(solution)/shard_map/all_gather | solution.py:17
Sparse Core Ops, SparseCore 0:
  30.0 74.5 all-gather.6
  106.7 79.9 all-gather.8
where the time goes:
time: 206 us; the launch traced here: 205 us
  waiting for transfers between devices  112 us (54%)
  blocking collectives  39.1 us (19%)
  between operations  14.9 us (7%)
  starting transfers between devices  14.5 us (7%)
  local copies, waits for them, and re-layouts  10.4 us (5%)
  other arithmetic  9.06 us (4%)
  matrix products  5.13 us (2%)
    all_gather x2, waiting for transfers between devices, entering(): gathered = jax.tree.map(lambda a: lax.all_gather(a, axis), part)  103 us
    unnamed x1, blocking collectives  22.7 us
    all_gather x1, blocking collectives, entering(): gathered = jax.tree.map(lambda a: lax.all_gather(a, axis), part)  16.4 us
    add x7, other arithmetic, chain_step(): following[0][:, None, None] * earlier[1] + following[1]  8.33 us
    all_to_all x1, waiting for transfers between devices, body(): lax.all_to_all(split_values, 'head', split_axis=1, concat_axis=0, tiled=T...  5.5 us
    unnamed x15, local copies, waits for them, and re-layouts  5.18 us
    all_to_all x1, starting transfers between devices, body(): lax.all_to_all(split_keys, 'head', split_axis=1, concat_axis=0, tiled=True)  4.24 us
  transfers between devices with their start and end apart: 6, of which 4 were waited for; matrix products, arithmetic and copies ran while one was open for 4% of the time, Pallas kernels for 0%

commit v1 on v0

v1 whole, which is shorter than its diff:
```python
import functools

import jax
import jax.numpy as jnp
from jax import lax
from jax.experimental import pallas as pl
from jax.experimental.pallas import tpu as pltpu
from jax.sharding import PartitionSpec as P

HEAD_COUNT = 32
DH = 128
SLOW = 4
CHUNK_HEADS = 2
LAG = 1
TAIL = 1

MESH = pl.DeviceIdType.MESH
F32 = jnp.float32
BF16 = jnp.bfloat16
EXACT = lax.Precision.HIGHEST


def dot_nn(x, y):
    return lax.dot_general(x, y, (((1,), (0,)), ((), ())), preferred_element_type=F32)


def dot_nt(x, y):
    return lax.dot_general(x, y, (((1,), (1,)), ((), ())), preferred_element_type=F32)


def dot_tn(x, y):
    return lax.dot_general(x, y, (((0,), (0,)), ((), ())), preferred_element_type=F32)


def kernel(
    seq_size, head_size,
    q_ref, k_ref, v_ref, g_ref, gates_ref,
    gq_ref, gk_ref, gv_ref,
    rows, ends, gain, table, grow, fade, inner, scaled_ref,
    local, reach, part_q, part_k, part_v,
    y_send, y_recv, n_send, n_recv, zp_send, zp_recv, zn_send, zn_recv,
    zgain,
    a2a_ssem, a2a_rsem, end_ssem, end_rsem,
    y_ssem, y_rsem, n_ssem, n_rsem, zp_ssem, zp_rsem, zn_ssem, zn_rsem,
):
    S, H = seq_size, head_size
    A = SLOW
    B = S // A
    RD = q_ref.shape[0]
    T = RD * H
    CW = q_ref.shape[1] // H
    NH = CW // DH
    HC = CHUNK_HEADS
    NC = NH // HC
    CC = HC * DH
    me_s = lax.axis_index("seq")
    me_h = lax.axis_index("head")
    a = me_s // B
    b = me_s % B
    lo = a * B
    hi = lo + B

    barrier = pltpu.get_barrier_semaphore()
    for r in range(1, H):
        pl.semaphore_signal(
            barrier, inc=1, device_id={"head": (me_h + r) % H}, device_id_type=MESH
        )

    @pl.loop(1, S)
    def _(r):
        pl.semaphore_signal(
            barrier, inc=1, device_id={"seq": (me_s + r) % S}, device_id_type=MESH
        )

    t_at = lax.broadcasted_iota(jnp.int32, (T, T), 0)
    s_at = lax.broadcasted_iota(jnp.int32, (T, T), 1)
    causal = t_at >= s_at
    tri = jnp.where(causal, 1.0, 0.0).astype(F32)
    gates = gates_ref[...]
    c_col = lax.dot_general(
        tri, gates, (((1,), (0,)), ((), ())), precision=EXACT, preferred_element_type=F32
    )
    c_row = c_col.T
    e_col = c_row[:, T - 1 : T]
    norm_col = jnp.sum(jnp.exp(e_col - c_row), axis=1, keepdims=True)
    ends[me_s, 0] = jnp.broadcast_to(norm_col, (NH, DH))
    ends[me_s, 1] = jnp.broadcast_to(e_col, (NH, DH))

    pl.semaphore_wait(barrier, (H - 1) + (S - 1))

    def end_copy(r, source, target):
        return pltpu.make_async_remote_copy(
            src_ref=ends.at[source],
            dst_ref=ends.at[source],
            send_sem=end_ssem.at[r - 1],
            recv_sem=end_rsem.at[r - 1],
            device_id={"seq": target},
            device_id_type=MESH,
        )

    @pl.loop(1, S)
    def _(r):
        end_copy(r, me_s, (me_s + r) % S).start()

    in_refs = (q_ref, k_ref, v_ref, g_ref)

    def a2a_copy(ch, r, t, source, target):
        return pltpu.make_async_remote_copy(
            src_ref=in_refs[t].at[:, pl.ds(pl.multiple_of(target * CW + ch * CC, CC), CC)],
            dst_ref=rows.at[
                t,
                pl.ds(pl.multiple_of(source * RD, RD), RD),
                pl.ds(pl.multiple_of(ch * CC, CC), CC),
            ],
            send_sem=a2a_ssem.at[ch, r - 1, t],
            recv_sem=a2a_rsem.at[ch, r - 1, t],
            device_id={"head": target},
            device_id_type=MESH,
        )

    @pl.loop(0, NC)
    def _(ch):
        for t in (1, 2, 0, 3):
            for r in range(1, H):
                a2a_copy(ch, r, t, me_h, (me_h + r) % H).start()

    own_rows = pl.ds(pl.multiple_of(me_h * RD, RD), RD)
    own_cols = pl.ds(pl.multiple_of(me_h * CW, CW), CW)
    for t in range(4):
        rows[t, own_rows, :] = in_refs[t][:, own_cols]

    @pl.when(a == 0)
    def _():
        y_recv[...] = jnp.zeros_like(y_recv)

    @pl.when(a == A - 1)
    def _():
        n_recv[...] = jnp.zeros_like(n_recv)

    for h in range(NH):
        col = c_col[:, h : h + 1]
        row = c_row[h : h + 1, :]
        decay = jnp.where(causal, jnp.exp(jnp.where(causal, col - row, 0.0)), 0.0)
        table[h] = decay
        grow[h] = jnp.broadcast_to(jnp.exp(col), (T, DH))
        fade[h] = jnp.broadcast_to(jnp.exp(c_col[T - 1 : T, h : h + 1] - col), (T, DH))
        inner[h] = jnp.broadcast_to(jnp.sum(decay, axis=1, keepdims=True), (T, DH))

    @pl.loop(1, S)
    def _(r):
        end_copy(r, (me_s + S - r) % S, me_s).wait_recv()

    zero = jnp.zeros((NH, DH), F32)

    def one_block(m, carry):
        pre, suf, norm = carry
        end = ends[m, 1]
        pre = pre + jnp.where((m >= lo) & (m < me_s), 1.0, 0.0) * end
        suf = suf + jnp.where((m > me_s) & (m < hi), 1.0, 0.0) * end
        earlier = jnp.where(m < me_s, 1.0, 0.0)
        norm = earlier * (norm * jnp.exp(end) + ends[m, 0]) + (1.0 - earlier) * norm
        return (pre, suf, norm)

    pre, suf, norm = lax.fori_loop(0, S, one_block, (zero, zero, zero))
    gain[0] = jnp.exp(pre)
    gain[1] = jnp.exp(suf)
    gain[2] = jnp.exp(pre + suf + ends[me_s, 1])
    gain[3] = norm

    @pl.loop(0, B - 1)
    def _(p):
        other = lo + (b + p + 1) % B

        def one_end(m, carry):
            pre, suf, between = carry
            end = ends[m, 1]
            pre = pre + jnp.where((m >= lo) & (m < other), 1.0, 0.0) * end
            suf = suf + jnp.where((m > other) & (m < hi), 1.0, 0.0) * end
            inside = (m > jnp.minimum(me_s, other)) & (m < jnp.maximum(me_s, other))
            between = between + jnp.where(inside, 1.0, 0.0) * end
            return (pre, suf, between)

        pre, suf, between = lax.fori_loop(0, S, one_end, (zero, zero, zero))
        zgain[p, 0] = jnp.exp(pre)
        zgain[p, 1] = jnp.where(other > me_s, 1.0, 0.0) * jnp.exp(between)
        zgain[p, 2] = jnp.exp(suf)
        zgain[p, 3] = jnp.where(other < me_s, 1.0, 0.0) * jnp.exp(between)

    def chain_copy(send, recv, ssem, rsem, m, target):
        return pltpu.make_async_remote_copy(
            src_ref=send.at[m],
            dst_ref=recv.at[m],
            send_sem=ssem.at[m],
            recv_sem=rsem.at[m],
            device_id={"seq": target},
            device_id_type=MESH,
        )

    def y_copy(m, target):
        return chain_copy(y_send, y_recv, y_ssem, y_rsem, m, target)

    def n_copy(m, target):
        return chain_copy(n_send, n_recv, n_ssem, n_rsem, m, target)

    def z_copy(send, recv, ssem, rsem, p, m, target):
        return pltpu.make_async_remote_copy(
            src_ref=send.at[p, m],
            dst_ref=recv.at[p, m],
            send_sem=ssem.at[p, m],
            recv_sem=rsem.at[p, m],
            device_id={"seq": target},
            device_id_type=MESH,
        )

    def zp_copy(p, m, target):
        return z_copy(zp_send, zp_recv, zp_ssem, zp_rsem, p, m, target)

    def zn_copy(p, m, target):
        return z_copy(zn_send, zn_recv, zn_ssem, zn_rsem, p, m, target)

    def peer(p):
        return lo + (b + p + 1) % B

    def source_peer(p):
        return lo + (b + B - p - 1) % B

    up = (me_s + B) % S
    down = (me_s + S - B) % S

    def weight(index, h):
        return gain[index, pl.ds(h, 1), :]

    def columns(h):
        return pl.ds(pl.multiple_of(h * DH, DH), DH)

    def arrive(m):
        for r in range(1, H):
            for t in range(4):
                a2a_copy(m, r, t, (me_h + H - r) % H, me_h).wait_recv()

    def states(m):
        for j in range(HC):
            h = m * HC + j
            at = columns(h)
            growth = grow[h]
            inverse = lax.rsqrt(growth * weight(3, h) + inner[h])
            inner[h] = inverse
            scaled = (rows[3, :, at].astype(F32) * inverse).astype(BF16)
            scaled_ref[h] = scaled
            key_fade = (rows[1, :, at].astype(F32) * fade[h]).astype(BF16)
            local[h] = dot_tn(key_fade, rows[2, :, at])
            query_growth = (rows[0, :, at].astype(F32) * growth).astype(BF16)
            reach[h] = dot_tn(query_growth, scaled)

    def within(m):
        for j in range(HC):
            h = m * HC + j
            at = columns(h)
            q, k, v, g = rows[0, :, at], rows[1, :, at], rows[2, :, at], rows[3, :, at]
            decay = table[h]
            weighted = (dot_nt(g, v) * decay * inner[h]).astype(BF16)
            affinity = (dot_nt(q, k) * decay).astype(BF16)
            part_q[h] = dot_nn(weighted, k)
            part_k[h] = dot_tn(weighted, q)
            part_v[h] = dot_tn(affinity, scaled_ref[h])

    def hop_up(m):
        @pl.when(a > 0)
        def _():
            y_copy(m, up).wait_recv()

        @pl.when(a < A - 1)
        def _():
            for j in range(HC):
                h = m * HC + j
                y_send[m, j] = (
                    weight(1, h) * local[h] + weight(2, h) * y_recv[m, j].astype(F32)
                ).astype(BF16)
            y_copy(m, up).start()

        @pl.loop(0, B - 1)
        def _(p):
            for j in range(HC):
                h = m * HC + j
                zp_send[p, m, j] = (
                    zgain[p, 0, pl.ds(h, 1), :] * y_recv[m, j].astype(F32)
                    + zgain[p, 1, pl.ds(h, 1), :] * local[h]
                ).astype(BF16)
            zp_copy(p, m, peer(p)).start()

    def hop_down(m):
        @pl.when(a < A - 1)
        def _():
            n_copy(m, down).wait_recv()

        @pl.when(a > 0)
        def _():
            for j in range(HC):
                h = m * HC + j
                n_send[m, j] = (
                    weight(0, h) * reach[h] + weight(2, h) * n_recv[m, j].astype(F32)
                ).astype(BF16)
            n_copy(m, down).start()

        @pl.loop(0, B - 1)
        def _(p):
            for j in range(HC):
                h = m * HC + j
                zn_send[p, m, j] = (
                    zgain[p, 2, pl.ds(h, 1), :] * n_recv[m, j].astype(F32)
                    + zgain[p, 3, pl.ds(h, 1), :] * reach[h]
                ).astype(BF16)
            zn_copy(p, m, peer(p)).start()

    def finish(m):
        @pl.loop(0, B - 1)
        def _(p):
            zp_copy(p, m, source_peer(p)).wait_recv()
            zn_copy(p, m, source_peer(p)).wait_recv()

        for j in range(HC):
            h = m * HC + j
            at = columns(h)
            prefix = weight(0, h) * y_recv[m, j].astype(F32)
            later = weight(1, h) * n_recv[m, j].astype(F32)
            prefix, later = lax.fori_loop(
                0,
                B - 1,
                lambda p, both: (
                    both[0] + zp_recv[p, m, j].astype(F32),
                    both[1] + zn_recv[p, m, j].astype(F32),
                ),
                (prefix, later),
            )
            prefix, later = prefix.astype(BF16), later.astype(BF16)
            gq = part_q[h] + grow[h] * dot_nt(scaled_ref[h], prefix)
            gk = part_k[h] + fade[h] * dot_nt(rows[2, :, at], later)
            gv = part_v[h] + fade[h] * dot_nn(rows[1, :, at], later)
            gq_ref[:, at] = gq.astype(BF16)
            gk_ref[:, at] = gk.astype(BF16)
            gv_ref[:, at] = gv.astype(BF16)

    def guarded(do, m):
        @pl.when((m >= 0) & (m < NC))
        def _():
            do(m)

    @pl.loop(0, NC + LAG * (A - 1) + TAIL)
    def _(n):
        @pl.when(n < NC)
        def _():
            arrive(n)
            states(n)

        guarded(hop_up, n - LAG * a)
        guarded(hop_down, n - LAG * (A - 1 - a))

        @pl.when(n < NC)
        def _():
            within(n)

        guarded(finish, n - LAG * (A - 1) - TAIL)

    @pl.loop(1, S)
    def _(r):
        end_copy(r, me_s, (me_s + r) % S).wait_send()

    @pl.loop(0, NC)
    def _(m):
        for r in range(1, H):
            for t in range(4):
                a2a_copy(m, r, t, me_h, (me_h + r) % H).wait_send()

        @pl.when(a < A - 1)
        def _():
            y_copy(m, up).wait_send()

        @pl.when(a > 0)
        def _():
            n_copy(m, down).wait_send()

        @pl.loop(0, B - 1)
        def _(p):
            zp_copy(p, m, peer(p)).wait_send()
            zn_copy(p, m, peer(p)).wait_send()


def body(seq_size, head_size, queries, keys, values, grad_out, gates):
    S, H = seq_size, head_size
    B = S // SLOW
    RD, width = queries.shape
    T = RD * H
    CW = width // H
    NH = CW // DH
    HC = CHUNK_HEADS
    NC = NH // HC
    square = (NH, T, DH)
    state = (NH, DH, DH)
    message = (NC, HC, DH, DH)
    vmem = pltpu.VMEM
    dma = pltpu.SemaphoreType.DMA
    whole = pl.BlockSpec(memory_space=pltpu.VMEM)
    out = jax.ShapeDtypeStruct((T, CW), BF16)
    return pl.pallas_call(
        functools.partial(kernel, S, H),
        out_shape=(out, out, out),
        in_specs=[whole] * 5,
        out_specs=(whole, whole, whole),
        scratch_shapes=[
            vmem((4, T, CW), BF16),
            vmem((S, 2, NH, DH), F32),
            vmem((4, NH, DH), F32),
            vmem((NH, T, T), F32),
            vmem(square, F32),
            vmem(square, F32),
            vmem(square, F32),
            vmem(square, BF16),
            vmem(state, F32),
            vmem(state, F32),
            vmem(square, F32),
            vmem(square, F32),
            vmem(square, F32),
            vmem(message, BF16),
            vmem(message, BF16),
            vmem(message, BF16),
            vmem(message, BF16),
            vmem((B - 1,) + message, BF16),
            vmem((B - 1,) + message, BF16),
            vmem((B - 1,) + message, BF16),
            vmem((B - 1,) + message, BF16),
            vmem((B - 1, 4, NH, DH), F32),
            dma((NC, H - 1, 4)),
            dma((NC, H - 1, 4)),
            dma((S - 1,)),
            dma((S - 1,)),
            dma((NC,)),
            dma((NC,)),
            dma((NC,)),
            dma((NC,)),
            dma((B - 1, NC)),
            dma((B - 1, NC)),
            dma((B - 1, NC)),
            dma((B - 1, NC)),
        ],
        compiler_params=pltpu.CompilerParams(
            collective_id=0,
            has_side_effects=True,
            vmem_limit_bytes=(16 << 20) + (B - 1) * (1 << 20),
        ),
    )(queries, keys, values, grad_out, gates)


def solution(mesh):
    placed = (
        P(("seq", "head"), None),
        P(("seq", "head"), None),
        P(("seq", "head"), None),
        P(("seq", "head"), None),
        P("seq", "head"),
    )
    return jax.shard_map(
        functools.partial(body, mesh.shape["seq"], mesh.shape["head"]),
        mesh=mesh,
        in_specs=placed,
        out_specs=(P("seq", "head"), P("seq", "head"), P("seq", "head")),
        check_vma=False,
    )
```

time: 206 us -> 44 us (0.21)
  waiting for transfers between devices: 112 us -> 0 us
  blocking collectives: 39.1 us -> 0 us
  Pallas kernels: 0 us -> 36.4 us
  starting transfers between devices: 14.5 us -> 0 us
  between operations: 14.9 us -> 0.65 us
  other arithmetic: 9.06 us -> 0 us
  matrix products: 5.13 us -> 0 us
  local copies, waits for them, and re-layouts: 10.4 us -> 6.69 us
    all_gather x2 -> x0, waiting for transfers between devices: 103 us -> none  [entering(): gathered = jax.tree.map(lambda a: lax.all_gather(a, axis), part)]
    pallas_call x0 -> x1, Pallas kernels: none -> 36.4 us  [body(): pl.pallas_call(functools.partial(kernel, S, H), out_shape=(out, out, out)...]
    unnamed x1 -> x0, blocking collectives: 22.7 us -> none
    all_gather x1 -> x0, blocking collectives: 16.4 us -> none  [entering(): gathered = jax.tree.map(lambda a: lax.all_gather(a, axis), part)]
    all_to_all x4 -> x0, starting transfers between devices: 14.5 us -> none  [the longest x1 4.24 us: body(): lax.all_to_all(split_keys, 'head', split_axis=1, concat_axis=0, tiled=True)]
    all_to_all x4 -> x0, waiting for transfers between devices: 8.88 us -> none  [the longest x1 5.5 us: body(): lax.all_to_all(split_values, 'head', split_axis=1, concat_axis=0, tiled=T...]
    add x7 -> x0, other arithmetic: 8.33 us -> none  [chain_step(): following[0][:, None, None] * earlier[1] + following[1]]
    dot_general x9 -> x0, matrix products: 5.13 us -> none  [the longest x1 1.37 us: body(): jnp.einsum('thd,the->hde', query_growth, scaled.astype(jnp.float32), prec...]
  transfers between devices with their start and end apart: 6 -> 0, of which waited for: 4 -> 0; matrix products, arithmetic and copies ran while one was open for 4% -> 0% of each run, Pallas kernels for 0% -> 0%
where the time goes in v1:
time: 44 us; the launch traced here: 43.7 us
  Pallas kernels  36.4 us (83%)
  local copies, waits for them, and re-layouts  6.69 us (15%)
  between operations  0.65 us (1%)
    pallas_call x1, Pallas kernels, body(): pl.pallas_call(functools.partial(kernel, S, H), out_shape=(out, out, out)...  36.4 us
    unnamed x12, local copies, waits for them, and re-layouts  6.69 us

profile of v1, /device:TPU:0, one launch (start us, length us, event | category | flops | bytes accessed | tf_op | source)
XLA Modules:
  0.0 43.7 jit_solution(14046755327953297235)
XLA Ops:
  0.6 0.8 %copy.8.gates_ref = f32[128,8]{1,0:T(8,128)S(1)} copy(f32[128,8]{0,1:T(8,128)} %param.9) | data formatting | bytes 8192 | tf_op args[4]
  1.4 0.0 copy-start
  1.4 0.9 %copy-done = bf16[32,4096]{1,0:T(8,128)(2,1)S(1)} copy-done((bf16[32,4096]{1,0:T(8,128)(2,1)S(1)}, bf16[32,4096]{1,0:T(8,128)(2,1)}, u32[]{:S(2)}) %copy-start) | copy-done | bytes 262168
  2.4 0.0 copy-start.1
  2.4 0.9 %copy-done.1 = bf16[32,4096]{1,0:T(8,128)(2,1)S(1)} copy-done((bf16[32,4096]{1,0:T(8,128)(2,1)S(1)}, bf16[32,4096]{1,0:T(8,128)(2,1)}, u32[]{:S(2)}) %copy-start.1) | copy-done | bytes 262168
  3.3 0.0 copy-start.2
  3.3 0.9 %copy-done.2 = bf16[32,4096]{1,0:T(8,128)(2,1)S(1)} copy-done((bf16[32,4096]{1,0:T(8,128)(2,1)S(1)}, bf16[32,4096]{1,0:T(8,128)(2,1)}, u32[]{:S(2)}) %copy-start.2) | copy-done | bytes 262168
  4.3 0.0 copy-start.3
  4.3 0.9 %copy-done.3 = bf16[32,4096]{1,0:T(8,128)(2,1)S(1)} copy-done((bf16[32,4096]{1,0:T(8,128)(2,1)S(1)}, bf16[32,4096]{1,0:T(8,128)(2,1)}, u32[]{:S(2)}) %copy-start.3) | copy-done | bytes 262168
  5.2 36.4 %shard_map.76 = (bf16[128,1024]{1,0:T(8,128)(2,1)S(1)}, bf16[128,1024]{1,0:T(8,128)(2,1)S(1)}, bf16[128,1024]{1,0:T(8,128)(2,1)S(1)}) custom-call(bf16[32,4096]{1,0:T(8,128)(2,1)S(1)} %copy-done, bf16[32,4096]{1,0:T(8,128)(2,1)S(1)} %copy-done.1, bf16[32,4096]{1,0:T(8,128)(2,1)S(1)} %copy-done.2, bf16[32,4096]{1,0:T(8,128)(2,1)S(1)} %copy-done.3, ...), custom_call_target="tpu_custom_call" | custom-call | tf_op jit(solution)/shard_map/pallas_call | solution.py:404
  41.6 0.7 %copy.12 = bf16[128,1024]{1,0:T(8,128)(2,1)} copy(bf16[128,1024]{1,0:T(8,128)(2,1)S(1)} %get-tuple-element.6) | data formatting | bytes 524288
  42.3 0.7 %copy.13 = bf16[128,1024]{1,0:T(8,128)(2,1)} copy(bf16[128,1024]{1,0:T(8,128)(2,1)S(1)} %get-tuple-element.7) | data formatting | bytes 524288
  43.0 0.7 %copy.14 = bf16[128,1024]{1,0:T(8,128)(2,1)} copy(bf16[128,1024]{1,0:T(8,128)(2,1)S(1)} %get-tuple-element.8) | data formatting | bytes 524288
Async XLA Ops:
  1.4 0.9 %copy-start = (bf16[32,4096]{1,0:T(8,128)(2,1)S(1)}, bf16[32,4096]{1,0:T(8,128)(2,1)}, u32[]{:S(2)}) copy-start(bf16[32,4096]{1,0:T(8,128)(2,1)} %q_ref.1) | copy-start | bytes 786436
  2.4 0.9 %copy-start.1 = (bf16[32,4096]{1,0:T(8,128)(2,1)S(1)}, bf16[32,4096]{1,0:T(8,128)(2,1)}, u32[]{:S(2)}) copy-start(bf16[32,4096]{1,0:T(8,128)(2,1)} %k_ref.1) | copy-start | bytes 786436
  3.3 0.9 %copy-start.2 = (bf16[32,4096]{1,0:T(8,128)(2,1)S(1)}, bf16[32,4096]{1,0:T(8,128)(2,1)}, u32[]{:S(2)}) copy-start(bf16[32,4096]{1,0:T(8,128)(2,1)} %v_ref.1) | copy-start | bytes 786436
  4.3 0.9 %copy-start.3 = (bf16[32,4096]{1,0:T(8,128)(2,1)S(1)}, bf16[32,4096]{1,0:T(8,128)(2,1)}, u32[]{:S(2)}) copy-start(bf16[32,4096]{1,0:T(8,128)(2,1)} %g_ref.1) | copy-start | bytes 786436

commit v2 on v1

--- a/solution.py
+++ b/solution.py
@@ -10,9 +10,10 @@
 HEAD_COUNT = 32
 DH = 128
 SLOW = 4
-CHUNK_HEADS = 2
-LAG = 1
-TAIL = 1
+ROW_HEADS = 2
+CHUNK_HEADS = 1
+LAG = 2
+TAIL = 2
 
 MESH = pl.DeviceIdType.MESH
 F32 = jnp.float32
@@ -39,8 +40,8 @@
     rows, ends, gain, table, grow, fade, inner, scaled_ref,
     local, reach, part_q, part_k, part_v,
     y_send, y_recv, n_send, n_recv, zp_send, zp_recv, zn_send, zn_recv,
-    zgain,
-    a2a_ssem, a2a_rsem, end_ssem, end_rsem,
+    zgain, out_rows, staged,
+    in_sem, out_sem, own_sem, a2a_ssem, a2a_rsem, end_ssem, end_rsem,
     y_ssem, y_rsem, n_ssem, n_rsem, zp_ssem, zp_rsem, zn_ssem, zn_rsem,
 ):
     S, H = seq_size, head_size
@@ -52,7 +53,8 @@
     NH = CW // DH
     HC = CHUNK_HEADS
     NC = NH // HC
-    CC = HC * DH
+    RC = ROW_HEADS * DH
+    PER = ROW_HEADS // HC
     me_s = lax.axis_index("seq")
     me_h = lax.axis_index("head")
     a = me_s // B
@@ -60,6 +62,14 @@
     lo = a * B
     hi = lo + B
 
+    def in_copy(t):
+        return pltpu.make_async_copy(
+            (q_ref, k_ref, v_ref, g_ref)[t], staged.at[t], in_sem.at[t]
+        )
+
+    for t in range(4):
+        in_copy(t).start()
+
     barrier = pltpu.get_barrier_semaphore()
     for r in range(1, H):
         pl.semaphore_signal(
@@ -76,11 +86,10 @@
     s_at = lax.broadcasted_iota(jnp.int32, (T, T), 1)
     causal = t_at >= s_at
     tri = jnp.where(causal, 1.0, 0.0).astype(F32)
-    gates = gates_ref[...]
-    c_col = lax.dot_general(
-        tri, gates, (((1,), (0,)), ((), ())), precision=EXACT, preferred_element_type=F32
+    c_row = lax.dot_general(
+        gates_ref[...], tri, (((1,), (1,)), ((), ())), precision=EXACT, preferred_element_type=F32
     )
-    c_row = c_col.T
+    c_col = c_row.T
     e_col = c_row[:, T - 1 : T]
     norm_col = jnp.sum(jnp.exp(e_col - c_row), axis=1, keepdims=True)
     ends[me_s, 0] = jnp.broadcast_to(norm_col, (NH, DH))
@@ -102,15 +111,14 @@
     def _(r):
         end_copy(r, me_s, (me_s + r) % S).start()
 
-    in_refs = (q_ref, k_ref, v_ref, g_ref)
 
     def a2a_copy(ch, r, t, source, target):
         return pltpu.make_async_remote_copy(
-            src_ref=in_refs[t].at[:, pl.ds(pl.multiple_of(target * CW + ch * CC, CC), CC)],
+            src_ref=staged.at[t, :, pl.ds(pl.multiple_of(target * CW + ch * RC, RC), RC)],
             dst_ref=rows.at[
                 t,
                 pl.ds(pl.multiple_of(source * RD, RD), RD),
-                pl.ds(pl.multiple_of(ch * CC, CC), CC),
+                pl.ds(pl.multiple_of(ch * RC, RC), RC),
             ],
             send_sem=a2a_ssem.at[ch, r - 1, t],
             recv_sem=a2a_rsem.at[ch, r - 1, t],
@@ -118,7 +126,10 @@
             device_id_type=MESH,
         )
 
-    @pl.loop(0, NC)
+    for t in range(4):
+        in_copy(t).wait()
+
+    @pl.loop(0, NH // ROW_HEADS)
     def _(ch):
         for t in (1, 2, 0, 3):
             for r in range(1, H):
@@ -126,8 +137,13 @@
 
     own_rows = pl.ds(pl.multiple_of(me_h * RD, RD), RD)
     own_cols = pl.ds(pl.multiple_of(me_h * CW, CW), CW)
+    def own_copy(t):
+        return pltpu.make_async_copy(
+            staged.at[t, :, own_cols], rows.at[t, own_rows, :], own_sem.at[t]
+        )
+
     for t in range(4):
-        rows[t, own_rows, :] = in_refs[t][:, own_cols]
+        own_copy(t).start()
 
     @pl.when(a == 0)
     def _():
@@ -311,6 +327,12 @@
                     + zgain[p, 3, pl.ds(h, 1), :] * reach[h]
                 ).astype(BF16)
             zn_copy(p, m, peer(p)).start()
+
+    def out_copy(t, m):
+        at = pl.ds(pl.multiple_of(m * HC * DH, HC * DH), HC * DH)
+        return pltpu.make_async_copy(
+            out_rows.at[t, :, at], (gq_ref, gk_ref, gv_ref)[t].at[:, at], out_sem.at[t, m]
+        )
 
     def finish(m):
         @pl.loop(0, B - 1)
@@ -336,20 +358,28 @@
             gq = part_q[h] + grow[h] * dot_nt(scaled_ref[h], prefix)
             gk = part_k[h] + fade[h] * dot_nt(rows[2, :, at], later)
             gv = part_v[h] + fade[h] * dot_nn(rows[1, :, at], later)
-            gq_ref[:, at] = gq.astype(BF16)
-            gk_ref[:, at] = gk.astype(BF16)
-            gv_ref[:, at] = gv.astype(BF16)
+            out_rows[0, :, at] = gq.astype(BF16)
+            out_rows[1, :, at] = gk.astype(BF16)
+            out_rows[2, :, at] = gv.astype(BF16)
+        for t in range(3):
+            out_copy(t, m).start()
 
     def guarded(do, m):
         @pl.when((m >= 0) & (m < NC))
         def _():
             do(m)
 
+    for t in range(4):
+        own_copy(t).wait()
+
     @pl.loop(0, NC + LAG * (A - 1) + TAIL)
     def _(n):
+        @pl.when((n < NC) & (n % PER == 0))
+        def _():
+            arrive(n // PER)
+
         @pl.when(n < NC)
         def _():
-            arrive(n)
             states(n)
 
         guarded(hop_up, n - LAG * a)
@@ -365,12 +395,17 @@
     def _(r):
         end_copy(r, me_s, (me_s + r) % S).wait_send()
 
-    @pl.loop(0, NC)
+    @pl.loop(0, NH // ROW_HEADS)
     def _(m):
         for r in range(1, H):
             for t in range(4):
                 a2a_copy(m, r, t, me_h, (me_h + r) % H).wait_send()
 
+    @pl.loop(0, NC)
+    def _(m):
+        for t in range(3):
+            out_copy(t, m).wait()
+
         @pl.when(a < A - 1)
         def _():
             y_copy(m, up).wait_send()
@@ -383,6 +418,12 @@
         def _(p):
             zp_copy(p, m, peer(p)).wait_send()
             zn_copy(p, m, peer(p)).wait_send()
+
+
+def hand_over(x_ref, y_ref, z_ref, x_out, y_out, z_out):
+    x_out[...] = x_ref[...]
+    y_out[...] = y_ref[...]
+    z_out[...] = z_ref[...]
 
 
 def body(seq_size, head_size, queries, keys, values, grad_out, gates):
@@ -401,11 +442,11 @@
     dma = pltpu.SemaphoreType.DMA
     whole = pl.BlockSpec(memory_space=pltpu.VMEM)
     out = jax.ShapeDtypeStruct((T, CW), BF16)
-    return pl.pallas_call(
+    results = pl.pallas_call(
         functools.partial(kernel, S, H),
         out_shape=(out, out, out),
-        in_specs=[whole] * 5,
-        out_specs=(whole, whole, whole),
+        in_specs=[pl.BlockSpec(memory_space=pl.ANY)] * 4 + [whole],
+        out_specs=(pl.BlockSpec(memory_space=pl.ANY),) * 3,
         scratch_shapes=[
             vmem((4, T, CW), BF16),
             vmem((S, 2, NH, DH), F32),
@@ -429,8 +470,13 @@
             vmem((B - 1,) + message, BF16),
             vmem((B - 1,) + message, BF16),
             vmem((B - 1, 4, NH, DH), F32),
-            dma((NC, H - 1, 4)),
-            dma((NC, H - 1, 4)),
+            vmem((3, T, CW), BF16),
+            vmem((4, RD, width), BF16),
+            dma((4,)),
+            dma((3, NC)),
+            dma((4,)),
+            dma((NH // ROW_HEADS, H - 1, 4)),
+            dma((NH // ROW_HEADS, H - 1, 4)),
             dma((S - 1,)),
             dma((S - 1,)),
             dma((NC,)),
@@ -445,9 +491,16 @@
         compiler_params=pltpu.CompilerParams(
             collective_id=0,
             has_side_effects=True,
-            vmem_limit_bytes=(16 << 20) + (B - 1) * (1 << 20),
+            vmem_limit_bytes=60 << 20,
         ),
-    )(queries, keys, values, grad_out, gates)
+    )(queries, keys, values, grad_out, gates.T)
+    return pl.pallas_call(
+        hand_over,
+        out_shape=(out, out, out),
+        in_specs=[whole] * 3,
+        out_specs=(whole, whole, whole),
+        compiler_params=pltpu.CompilerParams(vmem_limit_bytes=60 << 20),
+    )(*results)
 
 
 def solution(mesh):

time: 44 us -> 39.2 us (0.89)
  local copies, waits for them, and re-layouts: 6.69 us -> 0 us
  Pallas kernels: 36.4 us -> 38.4 us
    unnamed x12 -> x0, local copies, waits for them, and re-layouts: 6.69 us -> none
    pallas_call x0 -> x1, Pallas kernels: none -> 2 us  [body(): pl.pallas_call(hand_over, out_shape=(out, out, out), in_specs=[whole] * 3...]
where the time goes in v2:
time: 39.2 us; the launch traced here: 39 us
  Pallas kernels  38.4 us (98%)
  between operations  0.64 us (2%)
    pallas_call x1, Pallas kernels, body(): pl.pallas_call(functools.partial(kernel, S, H), out_shape=(out, out, out)...  36.4 us
    pallas_call x1, Pallas kernels, body(): pl.pallas_call(hand_over, out_shape=(out, out, out), in_specs=[whole] * 3...  2 us

profile of v2, /device:TPU:0, one launch (start us, length us, event | category | flops | bytes accessed | tf_op | source)
XLA Modules:
  0.0 39.0 jit_solution(8377076735823365922)
XLA Ops:
  0.6 36.4 %shard_map.76 = (bf16[128,1024]{1,0:T(8,128)(2,1)}, bf16[128,1024]{1,0:T(8,128)(2,1)}, bf16[128,1024]{1,0:T(8,128)(2,1)}) custom-call(bf16[32,4096]{1,0:T(8,128)(2,1)} %q_ref.1, bf16[32,4096]{1,0:T(8,128)(2,1)} %k_ref.1, bf16[32,4096]{1,0:T(8,128)(2,1)} %v_ref.1, bf16[32,4096]{1,0:T(8,128)(2,1)} %g_ref.1, f32[8,128]{1,0:T(8,128)} %bitcast.1), custom_call_target="tpu_custom_call" | custom-call | tf_op jit(solution)/shard_map/pallas_call | solution.py:445
  37.0 2.0 %shard_map.77 = (bf16[128,1024]{1,0:T(8,128)(2,1)}, bf16[128,1024]{1,0:T(8,128)(2,1)}, bf16[128,1024]{1,0:T(8,128)(2,1)}) custom-call(bf16[128,1024]{1,0:T(8,128)(2,1)} %get-tuple-element.6.x_ref, bf16[128,1024]{1,0:T(8,128)(2,1)} %get-tuple-element.7.y_ref, bf16[128,1024]{1,0:T(8,128)(2,1)} %get-tuple-element.8.z_ref), custom_call_target="tpu_custom_call" | custom-call | tf_op jit(solution)/shard_map/pallas_call | solution.py:497

commit v3 on v2

--- a/solution.py
+++ b/solution.py
@@ -13,7 +13,8 @@
 ROW_HEADS = 2
 CHUNK_HEADS = 1
 LAG = 2
-TAIL = 2
+SPREAD = 1
+TAIL = 3
 
 MESH = pl.DeviceIdType.MESH
 F32 = jnp.float32
@@ -40,7 +41,8 @@
     rows, ends, gain, table, grow, fade, inner, scaled_ref,
     local, reach, part_q, part_k, part_v,
     y_send, y_recv, n_send, n_recv, zp_send, zp_recv, zn_send, zn_recv,
-    zgain, out_rows, staged,
+    zgain, out_rows, staged, dy_recv, dn_recv, sum_p, sum_n,
+    dy_ssem, dy_rsem, dn_ssem, dn_rsem,
     in_sem, out_sem, own_sem, a2a_ssem, a2a_rsem, end_ssem, end_rsem,
     y_ssem, y_rsem, n_ssem, n_rsem, zp_ssem, zp_rsem, zn_ssem, zn_rsem,
 ):
@@ -53,6 +55,7 @@
     NH = CW // DH
     HC = CHUNK_HEADS
     NC = NH // HC
+    first = NC - SPREAD
     RC = ROW_HEADS * DH
     PER = ROW_HEADS // HC
     me_s = lax.axis_index("seq")
@@ -81,6 +84,32 @@
         pl.semaphore_signal(
             barrier, inc=1, device_id={"seq": (me_s + r) % S}, device_id_type=MESH
         )
+
+    pl.semaphore_wait(barrier, (H - 1) + (S - 1))
+
+    def a2a_copy(ch, r, t, source, target):
+        return pltpu.make_async_remote_copy(
+            src_ref=staged.at[t, :, pl.ds(pl.multiple_of(target * CW + ch * RC, RC), RC)],
+            dst_ref=rows.at[
+                t,
+                pl.ds(pl.multiple_of(source * RD, RD), RD),
+                pl.ds(pl.multiple_of(ch * RC, RC), RC),
+            ],
+            send_sem=a2a_ssem.at[ch, r - 1, t],
+            recv_sem=a2a_rsem.at[ch, r - 1, t],
+            device_id={"head": target},
+            device_id_type=MESH,
+        )
+
+    for t in range(4):
+        in_copy(t).wait()
+
+    def send_rows(ch):
+        for t in (1, 2, 0, 3):
+            for r in range(1, H):
+                a2a_copy(ch, r, t, me_h, (me_h + r) % H).start()
+
+    send_rows(0)
 
     t_at = lax.broadcasted_iota(jnp.int32, (T, T), 0)
     s_at = lax.broadcasted_iota(jnp.int32, (T, T), 1)
@@ -95,8 +124,6 @@
     ends[me_s, 0] = jnp.broadcast_to(norm_col, (NH, DH))
     ends[me_s, 1] = jnp.broadcast_to(e_col, (NH, DH))
 
-    pl.semaphore_wait(barrier, (H - 1) + (S - 1))
-
     def end_copy(r, source, target):
         return pltpu.make_async_remote_copy(
             src_ref=ends.at[source],
@@ -112,28 +139,9 @@
         end_copy(r, me_s, (me_s + r) % S).start()
 
 
-    def a2a_copy(ch, r, t, source, target):
-        return pltpu.make_async_remote_copy(
-            src_ref=staged.at[t, :, pl.ds(pl.multiple_of(target * CW + ch * RC, RC), RC)],
-            dst_ref=rows.at[
-                t,
-                pl.ds(pl.multiple_of(source * RD, RD), RD),
-                pl.ds(pl.multiple_of(ch * RC, RC), RC),
-            ],
-            send_sem=a2a_ssem.at[ch, r - 1, t],
-            recv_sem=a2a_rsem.at[ch, r - 1, t],
-            device_id={"head": target},
-            device_id_type=MESH,
-        )
-
-    for t in range(4):
-        in_copy(t).wait()
-
-    @pl.loop(0, NH // ROW_HEADS)
+    @pl.loop(1, NH // ROW_HEADS)
     def _(ch):
-        for t in (1, 2, 0, 3):
-            for r in range(1, H):
-                a2a_copy(ch, r, t, me_h, (me_h + r) % H).start()
+        send_rows(ch)
 
     own_rows = pl.ds(pl.multiple_of(me_h * RD, RD), RD)
     own_cols = pl.ds(pl.multiple_of(me_h * CW, CW), CW)
@@ -148,10 +156,12 @@
     @pl.when(a == 0)
     def _():
         y_recv[...] = jnp.zeros_like(y_recv)
+        dy_recv[...] = jnp.zeros_like(dy_recv)
 
     @pl.when(a == A - 1)
     def _():
         n_recv[...] = jnp.zeros_like(n_recv)
+        dn_recv[...] = jnp.zeros_like(dn_recv)
 
     for h in range(NH):
         col = c_col[:, h : h + 1]
@@ -233,6 +243,24 @@
 
     def zn_copy(p, m, target):
         return z_copy(zn_send, zn_recv, zn_ssem, zn_rsem, p, m, target)
+
+    def spread_copy(send, recv, ssem, rsem, p, m, target):
+        return pltpu.make_async_remote_copy(
+            src_ref=send.at[m],
+            dst_ref=recv.at[p, m - first],
+            send_sem=ssem.at[p, m - first],
+            recv_sem=rsem.at[p, m - first],
+            device_id={"seq": target},
+            device_id_type=MESH,
+        )
+
+    def dy_copy(p, m):
+        target = (peer(p) + B) % S
+        return spread_copy(y_send, dy_recv, dy_ssem, dy_rsem, p, m, target)
+
+    def dn_copy(p, m):
+        target = (peer(p) + S - B) % S
+        return spread_copy(n_send, dn_recv, dn_ssem, dn_rsem, p, m, target)
 
     def peer(p):
         return lo + (b + p + 1) % B
@@ -280,6 +308,16 @@
             part_k[h] = dot_tn(weighted, q)
             part_v[h] = dot_tn(affinity, scaled_ref[h])
 
+    def early(m):
+        @pl.loop(0, B - 1)
+        def _(p):
+            for j in range(HC):
+                h = m * HC + j
+                zp_send[p, m, j] = (zgain[p, 1, pl.ds(h, 1), :] * local[h]).astype(BF16)
+                zn_send[p, m, j] = (zgain[p, 3, pl.ds(h, 1), :] * reach[h]).astype(BF16)
+            zp_copy(p, m, peer(p)).start()
+            zn_copy(p, m, peer(p)).start()
+
     def hop_up(m):
         @pl.when(a > 0)
         def _():
@@ -294,7 +332,13 @@
                 ).astype(BF16)
             y_copy(m, up).start()
 
-        @pl.loop(0, B - 1)
+            @pl.when(m >= first)
+            def _():
+                @pl.loop(0, B - 1)
+                def _(p):
+                    dy_copy(p, m).start()
+
+        @pl.loop(0, jnp.where(m < first, B - 1, 0))
         def _(p):
             for j in range(HC):
                 h = m * HC + j
@@ -318,7 +362,13 @@
                 ).astype(BF16)
             n_copy(m, down).start()
 
-        @pl.loop(0, B - 1)
+            @pl.when(m >= first)
+            def _():
+                @pl.loop(0, B - 1)
+                def _(p):
+                    dn_copy(p, m).start()
+
+        @pl.loop(0, jnp.where(m < first, B - 1, 0))
         def _(p):
             for j in range(HC):
                 h = m * HC + j
@@ -341,10 +391,30 @@
             zn_copy(p, m, source_peer(p)).wait_recv()
 
         for j in range(HC):
+            sum_p[j] = y_recv[m, j].astype(F32)
+            sum_n[j] = n_recv[m, j].astype(F32)
+
+        @pl.when(m >= first)
+        def _():
+            @pl.loop(0, B - 1)
+            def _(p):
+                @pl.when(a > 0)
+                def _():
+                    dy_copy(p, m).wait_recv()
+
+                @pl.when(a < A - 1)
+                def _():
+                    dn_copy(p, m).wait_recv()
+
+                for j in range(HC):
+                    sum_p[j] += dy_recv[p, m - first, j].astype(F32)
+                    sum_n[j] += dn_recv[p, m - first, j].astype(F32)
+
+        for j in range(HC):
             h = m * HC + j
             at = columns(h)
-            prefix = weight(0, h) * y_recv[m, j].astype(F32)
-            later = weight(1, h) * n_recv[m, j].astype(F32)
+            prefix = weight(0, h) * sum_p[j]
+            later = weight(1, h) * sum_n[j]
             prefix, later = lax.fori_loop(
                 0,
                 B - 1,
@@ -382,6 +452,10 @@
         def _():
             states(n)
 
+        @pl.when((n >= first) & (n < NC))
+        def _():
+            early(n)
+
         guarded(hop_up, n - LAG * a)
         guarded(hop_down, n - LAG * (A - 1 - a))
 
@@ -414,16 +488,35 @@
         def _():
             n_copy(m, down).wait_send()
 
+        @pl.when(m >= first)
+        def _():
+            @pl.loop(0, B - 1)
+            def _(p):
+                @pl.when(a < A - 1)
+                def _():
+                    dy_copy(p, m).wait_send()
+
+                @pl.when(a > 0)
+                def _():
+                    dn_copy(p, m).wait_send()
+
         @pl.loop(0, B - 1)
         def _(p):
             zp_copy(p, m, peer(p)).wait_send()
             zn_copy(p, m, peer(p)).wait_send()
 
 
-def hand_over(x_ref, y_ref, z_ref, x_out, y_out, z_out):
-    x_out[...] = x_ref[...]
-    y_out[...] = y_ref[...]
-    z_out[...] = z_ref[...]
+def hand_over(x_ref, y_ref, z_ref, x_out, y_out, z_out, held, in_sems, out_sems):
+    sources, targets = (x_ref, y_ref, z_ref), (x_out, y_out, z_out)
+    loads = [pltpu.make_async_copy(sources[i], held.at[i], in_sems.at[i]) for i in range(3)]
+    stores = [pltpu.make_async_copy(held.at[i], targets[i], out_sems.at[i]) for i in range(3)]
+    for load in loads:
+        load.start()
+    for load, store in zip(loads, stores):
+        load.wait()
+        store.start()
+    for store in stores:
+        store.wait()
 
 
 def body(seq_size, head_size, queries, keys, values, grad_out, gates):
@@ -472,6 +565,14 @@
             vmem((B - 1, 4, NH, DH), F32),
             vmem((3, T, CW), BF16),
             vmem((4, RD, width), BF16),
+            vmem((B - 1, SPREAD, HC, DH, DH), BF16),
+            vmem((B - 1, SPREAD, HC, DH, DH), BF16),
+            vmem((HC, DH, DH), F32),
+            vmem((HC, DH, DH), F32),
+            dma((B - 1, SPREAD)),
+            dma((B - 1, SPREAD)),
+            dma((B - 1, SPREAD)),
+            dma((B - 1, SPREAD)),
             dma((4,)),
             dma((3, NC)),
             dma((4,)),
@@ -497,8 +598,9 @@
     return pl.pallas_call(
         hand_over,
         out_shape=(out, out, out),
-        in_specs=[whole] * 3,
-        out_specs=(whole, whole, whole),
+        in_specs=[pl.BlockSpec(memory_space=pl.ANY)] * 3,
+        out_specs=(pl.BlockSpec(memory_space=pl.ANY),) * 3,
+        scratch_shapes=[vmem((3, T, CW), BF16), dma((3,)), dma((3,))],
         compiler_params=pltpu.CompilerParams(vmem_limit_bytes=60 << 20),
     )(*results)
 

time: 39.2 us -> 38.6 us (0.985)
  Pallas kernels: 38.4 us -> 37.7 us
    pallas_call x1, Pallas kernels: 36.4 us -> 35.9 us  [body(): pl.pallas_call(functools.partial(kernel, S, H), out_shape=(out, out, out)...]
where the time goes in v3:
time: 38.6 us; the launch traced here: 38.4 us
  Pallas kernels  37.7 us (98%)
  between operations  0.64 us (2%)
    pallas_call x1, Pallas kernels, body(): pl.pallas_call(functools.partial(kernel, S, H), out_shape=(out, out, out)...  35.9 us
    pallas_call x1, Pallas kernels, body(): pl.pallas_call(hand_over, out_shape=(out, out, out), in_specs=[pl.BlockSp...  1.88 us

profile of v3, /device:TPU:0, one launch (start us, length us, event | category | flops | bytes accessed | tf_op | source)
XLA Modules:
  0.0 38.4 jit_solution(5560577740687822944)
XLA Ops:
  0.6 35.9 %shard_map.76 = (bf16[128,1024]{1,0:T(8,128)(2,1)}, bf16[128,1024]{1,0:T(8,128)(2,1)}, bf16[128,1024]{1,0:T(8,128)(2,1)}) custom-call(bf16[32,4096]{1,0:T(8,128)(2,1)} %q_ref.1, bf16[32,4096]{1,0:T(8,128)(2,1)} %k_ref.1, bf16[32,4096]{1,0:T(8,128)(2,1)} %v_ref.1, bf16[32,4096]{1,0:T(8,128)(2,1)} %g_ref.1, f32[8,128]{1,0:T(8,128)} %bitcast.1), custom_call_target="tpu_custom_call" | custom-call | tf_op jit(solution)/shard_map/pallas_call | solution.py:538
  36.5 1.9 %shard_map.77 = (bf16[128,1024]{1,0:T(8,128)(2,1)}, bf16[128,1024]{1,0:T(8,128)(2,1)}, bf16[128,1024]{1,0:T(8,128)(2,1)}) custom-call(bf16[128,1024]{1,0:T(8,128)(2,1)} %get-tuple-element.6.x_ref, bf16[128,1024]{1,0:T(8,128)(2,1)} %get-tuple-element.7.y_ref, bf16[128,1024]{1,0:T(8,128)(2,1)} %get-tuple-element.8.z_ref), custom_call_target="tpu_custom_call" | custom-call | tf_op jit(solution)/shard_map/pallas_call | solution.py:598
